TPU v7x, 32 devices: a whole 2x2x4 slice. The times are simulated.
32 devices in a mesh: gx: 8 (over z, core), gy: 4 (over y, x).
Axes of the slice: x: 2, y: 2, z: 4, core: 2. Of those that a mesh axis runs over, the one named last changes fastest.
Arguments:
- points: bfloat16 [64, 65536], P(None, ('gx', 'gy')), may hold values from -6 to 6
- vectors: bfloat16 [32, 65536], P(None, ('gx', 'gy')), may hold values from -6 to 6
- leaf_pick: int32 [128, 128], P(('gx', 'gy')), may hold values from 0 to 511
- leaf_assign: int32 [128, 512], P(('gx', 'gy')), may hold values from 0 to 127
- device_pick: int32 [32, 128], P(('gx', 'gy')), may hold values from 0 to 511
- device_assign: int32 [32, 512], P(('gx', 'gy')), may hold values from 0 to 127
- node_pick: int32 [8, 3, 128], P('gx'), may hold values from 0 to 255
- node_assign: int32 [8, 3, 256], P('gx'), may hold values from 0 to 127
- far_mask: int32 [8, 8], P('gx'), may hold values from 0 to 1, as said below
- near_lower: int32 [32, 4, 12], P(('gx', 'gy')), may hold values from -1 to 3, as said below
- near_upper: int32 [32, 4, 12], P(('gx', 'gy')), may hold values from 0 to 3, as said below
Outputs:
- potential: float32 [32, 65536], P(None, ('gx', 'gy'))
Inputs may be any that keep to these rules, and one draw needn't show every extreme that they name: near_lower[d, o, j] is a local leaf of device d forming a near pair with local leaf near_upper[d, o, j] of device d + o + 1, or -1 for an empty slot; the slots of one d and o never name the same pair of leaves, and no live slot names a device past the last. `near_upper`: A local leaf of device d + o + 1, read only where near_lower is live. `far_mask`: Symmetric, zero on the diagonal, one where the two group indices differ by exactly 1.
All inputs are finite; a program needn't handle non-finite values.
Results may differ from a plain program's by a relative error of at most 0.0015.
Values may be sent and summed in bfloat16 or wider, within the bound.
No kernel may reach another device: no remote copies, remote signals or barrier semaphores. Data moves between devices by JAX's collectives and lax.ppermute only.
A program may use at most 128 MiB of HBM per device.

v0:
```python
import jax
import jax.numpy as jnp
from jax import lax
from jax.sharding import PartitionSpec as P

DIM = 64
COLS = 32
LEAF = 512
SKEL = 128
LPD = 4
KERNEL_RATE = 2.0


def passed_along(value, axis, steps):
    count = lax.axis_size(axis)
    first, last = (max(0, -steps), min(count, count - steps))
    return lax.ppermute(value, axis, [(source, source + steps) for source in range(first, last)])


def from_partner(value, axis, bit):
    mask = 2**bit
    pairs = [(source, source ^ mask) for source in range(lax.axis_size(axis))]
    return lax.ppermute(value, axis, pairs)


def kernel_block(source, target):
    decay_rate = KERNEL_RATE / source.shape[0]
    source_wide = source.astype(jnp.float32)
    target_wide = target.astype(jnp.float32)
    source_norm = jnp.sum(source_wide * source_wide, axis=0)
    target_norm = jnp.sum(target_wide * target_wide, axis=0)
    products = lax.dot_general(
        source, target, (((0,), (0,)), ((), ())), preferred_element_type=jnp.float32
    )
    return jnp.exp(-decay_rate * (source_norm[:, None] + target_norm[None, :] - 2.0 * products))


def add_columns(running, terms, first_col):
    current = lax.dynamic_slice_in_dim(running, first_col, terms.shape[1], 1)
    return lax.dynamic_update_slice_in_dim(running, current + terms, first_col, 1)


def pick_columns(table_matrix, col_index):
    return jnp.take(table_matrix, col_index, axis=1)


def one_hot(assignment, width_count):
    return (assignment[:, None] == jnp.arange(width_count, dtype=jnp.int32)[None, :]).astype(
        jnp.float32
    )


def pair_terms(low_points, low_values, high_points, high_values):
    kernel_tile = kernel_block(low_points, high_points).astype(jnp.bfloat16)
    to_upper = jnp.dot(low_values, kernel_tile, preferred_element_type=jnp.float32)
    to_lower = lax.dot_general(
        high_values, kernel_tile, (((1,), (1,)), ((), ())), preferred_element_type=jnp.float32
    )
    return (to_lower, to_upper)


def neighbour_terms(
    offset,
    near_lower,
    near_upper,
    points,
    columns,
    high_block,
    high_columns,
    near_terms,
    upper_terms,
):
    for slot_index in range(near_lower.shape[2]):
        lower_leaf = near_lower[0, offset - 1, slot_index]
        upper_leaf = near_upper[0, offset - 1, slot_index]
        live_flag = lower_leaf >= 0
        lower_col = jnp.maximum(lower_leaf, 0) * LEAF
        upper_col = upper_leaf * LEAF
        low_points = lax.dynamic_slice_in_dim(points, lower_col, LEAF, 1)
        low_values = lax.dynamic_slice_in_dim(columns, lower_col, LEAF, 1)
        high_points = lax.dynamic_slice_in_dim(high_block, upper_col, LEAF, 1)
        high_values = lax.dynamic_slice_in_dim(high_columns, upper_col, LEAF, 1)
        to_lower, to_upper = pair_terms(low_points, low_values, high_points, high_values)
        live_scale = live_flag.astype(jnp.float32)
        to_lower = to_lower * live_scale
        to_upper = to_upper * live_scale
        near_terms = add_columns(near_terms, to_lower, lower_col)
        upper_terms = add_columns(upper_terms, to_upper, upper_col)
    return (near_terms, upper_terms)


def on_device(
    points,
    vectors,
    leaf_pick,
    leaf_assign,
    device_pick,
    device_assign,
    node_pick,
    node_assign,
    far_mask,
    near_lower,
    near_upper,
):
    device_cols = points.shape[1]
    reach_count = lax.axis_size("gy")
    levels = reach_count.bit_length() - 1
    row_index = lax.axis_index("gy")

    def self_target(target, running):
        first_col = target * LEAF
        target_points = lax.dynamic_slice_in_dim(points, first_col, LEAF, 1)
        kernel_tile = kernel_block(points, target_points).astype(jnp.bfloat16)
        self_terms = jnp.dot(vectors, kernel_tile, preferred_element_type=jnp.float32)
        return lax.dynamic_update_slice_in_dim(running, self_terms, first_col, 1)

    near_terms = lax.fori_loop(0, LPD, self_target, jnp.zeros((COLS, device_cols), jnp.float32))
    for offset in range(1, reach_count + 1):
        high_block, high_columns = passed_along((points, vectors), ("gx", "gy"), -offset)
        upper_terms = jnp.zeros((COLS, device_cols), jnp.float32)
        near_terms, upper_terms = neighbour_terms(
            offset,
            near_lower,
            near_upper,
            points,
            vectors,
            high_block,
            high_columns,
            near_terms,
            upper_terms,
        )
        near_terms = near_terms + passed_along(upper_terms, ("gx", "gy"), offset)
    leaf_points = points.reshape(DIM, LPD, LEAF)
    leaf_values = vectors.reshape(COLS, LPD, LEAF)
    skeleton_points = jax.vmap(pick_columns, in_axes=(1, 0))(leaf_points, leaf_pick)
    leaf_onehot = leaf_assign[:, :, None] == jnp.arange(SKEL, dtype=jnp.int32)[None, None, :]
    leaf_weights = jnp.einsum(
        "cln,lns->lcs",
        leaf_values,
        leaf_onehot.astype(jnp.bfloat16),
        preferred_element_type=jnp.float32,
    )
    joined_points = skeleton_points.transpose(1, 0, 2).reshape(DIM, LPD * SKEL)
    joined_weights = leaf_weights.transpose(1, 0, 2).reshape(COLS, LPD * SKEL)
    node_points = jnp.take(joined_points, device_pick[0], axis=1)
    device_onehot = one_hot(device_assign[0], SKEL)
    node_weights = jnp.dot(joined_weights, device_onehot, precision=lax.Precision.HIGHEST)
    path_onehots = []
    for level_index in range(1, levels + 1):
        heap_index = (reach_count >> level_index) - 1 + (row_index >> level_index)
        assignment = lax.dynamic_index_in_dim(node_assign[0], heap_index, 0, keepdims=False)
        path_onehots.append(one_hot(assignment, SKEL))
    for level_index in range(1, levels + 1):
        bit_index = level_index - 1
        other_points = from_partner(node_points, "gy", bit_index)
        other_weights = from_partner(node_weights, "gy", bit_index)
        upper_side = row_index >> bit_index & 1 == 1
        pair_points = jnp.where(
            upper_side,
            jnp.concatenate([other_points, node_points], 1),
            jnp.concatenate([node_points, other_points], 1),
        )
        pair_weights = jnp.where(
            upper_side,
            jnp.concatenate([other_weights, node_weights], 1),
            jnp.concatenate([node_weights, other_weights], 1),
        )
        heap_index = (reach_count >> level_index) - 1 + (row_index >> level_index)
        node_picks = lax.dynamic_index_in_dim(node_pick[0], heap_index, 0, keepdims=False)
        node_points = jnp.take(pair_points, node_picks, axis=1)
        node_weights = jnp.dot(
            pair_weights, path_onehots[level_index - 1], precision=lax.Precision.HIGHEST
        )
    gathered_roots = lax.all_gather(node_points[None], "gx", axis=0, tiled=True)
    far_flags = far_mask[0].astype(jnp.float32)
    root_kernels = jax.vmap(kernel_block, in_axes=(0, None))(gathered_roots, node_points)
    node_potential = jnp.einsum(
        "n,ncs,nst->ct",
        far_flags,
        lax.all_gather(node_weights[None], "gx", axis=0, tiled=True),
        root_kernels,
        precision=lax.Precision.HIGHEST,
    )
    for level_index in range(levels, 0, -1):
        child_potential = jnp.dot(
            node_potential, path_onehots[level_index - 1].T, precision=lax.Precision.HIGHEST
        )
        child_side = row_index >> level_index - 1 & 1
        node_potential = lax.dynamic_slice_in_dim(child_potential, child_side * SKEL, SKEL, 1)
    leaf_joined = jnp.dot(node_potential, device_onehot.T, precision=lax.Precision.HIGHEST).reshape(
        COLS, LPD, SKEL
    )
    far_terms = jnp.einsum(
        "cls,lns->cln",
        leaf_joined,
        leaf_onehot.astype(jnp.float32),
        precision=lax.Precision.HIGHEST,
    ).reshape(COLS, device_cols)
    return near_terms + far_terms


def solution(mesh):
    placed = (
        P(None, ("gx", "gy")),
        P(None, ("gx", "gy")),
        P(("gx", "gy"), None),
        P(("gx", "gy"), None),
        P(("gx", "gy"), None),
        P(("gx", "gy"), None),
        P("gx", None, None),
        P("gx", None, None),
        P("gx", None),
        P(("gx", "gy"), None, None),
        P(("gx", "gy"), None, None),
    )
    return jax.shard_map(
        on_device, mesh=mesh, in_specs=placed, out_specs=P(None, ("gx", "gy")), check_vma=False
    )
```

profile of v0, /device:TPU:5, one launch (start us, length us, event | category | flops | bytes accessed | tf_op | source)
XLA Modules:
  0.0 233.5 jit_solution(3398589110747293190)
XLA Ops:
  0.0 3.2 %collective-permute-start.1 = (bf16[64,2048]{1,0:T(8,128)(2,1)}, bf16[64,2048]{1,0:T(8,128)(2,1)S(1)}, u32[]{:S(2)}, u32[]{:S(2)}) collective-permute-start(bf16[64,2048]{1,0:T(8,128)(2,1)} %param.15), channel_id=1, source_target_pairs={{1,0},{2,1},{3,2},{4,3},{5,4},{6,5},{7,6},{8,7},{9,8},{10,9},{11,1... | collective-permute-start | bytes 786440 | tf_op jit(solution)/shard_map/ppermute | solution.py:17
  3.2 3.7 %collective-permute-start.4 = (bf16[64,2048]{1,0:T(8,128)(2,1)}, bf16[64,2048]{1,0:T(8,128)(2,1)S(1)}, u32[]{:S(2)}, u32[]{:S(2)}) collective-permute-start(bf16[64,2048]{1,0:T(8,128)(2,1)} %param.15), channel_id=1, source_target_pairs={{2,0},{3,1},{4,2},{5,3},{6,4},{7,5},{8,6},{9,7},{10,8},{11,9},{12,... | collective-permute-start | bytes 786440 | tf_op jit(solution)/shard_map/ppermute | solution.py:17
  6.9 2.4 %collective-permute-start = (bf16[32,2048]{1,0:T(8,128)(2,1)}, bf16[32,2048]{1,0:T(8,128)(2,1)S(1)}, u32[]{:S(2)}, u32[]{:S(2)}) collective-permute-start(bf16[32,2048]{1,0:T(8,128)(2,1)} %param.16), channel_id=1, source_target_pairs={{1,0},{2,1},{3,2},{4,3},{5,4},{6,5},{7,6},{8,7},{9,8},{10,9},{11,1... | collective-permute-start | bytes 393224 | tf_op jit(solution)/shard_map/ppermute | solution.py:17
  9.4 1.9 collective-permute-start.3
  11.3 1.2 copy.24
  12.7 3.2 %gather_fusion.1 = bf16[512,64]{1,0:T(8,128)(2,1)S(1)} fusion(bf16[4,64,512]{1,2,0:T(8,128)(2,1)S(1)} %bitcast.341, s32[512]{0:T(512)S(1)} %fusion.383), kind=kCustom, calls=%fused_computation.3 | custom fusion | bytes 135168 | tf_op jit(solution)/shard_map/vmap(jit(_take))/gather | solution.py:44
  16.0 0.7 gather_fusion
  16.8 1.5 collective-permute-start.14
  18.3 0.7 fusion.396
  19.6 0.7 fusion.392
  22.3 0.7 fusion.393
  28.7 0.7 fusion.395
  52.0 0.7 fusion.394
  70.5 0.7 fusion.391
  112.8 6.5 %while.13 = (s32[]{:T(128)}, f32[32,2048]{1,0:T(8,128)S(1)}, bf16[64,2048]{1,0:T(8,128)(2,1)S(1)}, bf16[32,2048]{1,0:T(8,128)(2,1)S(1)}, s32[]{:T(128)}, /*index=5*/s32[]{:T(128)}, s32[]{:T(128)}, s32[]{:T(128)}) while((s32[]{:T(128)}, f32[32,2048]{1,0:T(8,128)S(1)}, bf16[64,2048]{1,0:T(8,128)(2,1)S(1)}, bf16[32,2048]{1,0:T(8,128)(2,1)S(1)}, ...), condition=%wide.region_3.0_spmd, body=%wide.region_0.0_spmd.sunk | while | flops 207058432 | bytes 873615 | solution.py:117
  113.0 1.5 fusion.505
  114.6 1.5 fusion.505
  116.2 1.5 fusion.505
  117.9 1.5 fusion.505
  119.6 0.7 convolution_bitcast_fusion.2
  122.3 0.7 gather_fusion.2
  123.1 1.7 collective-permute-done.12
  125.3 2.2 collective-permute-done.15
  127.6 0.7 collective-permute-start.13
  128.3 0.7 gather_fusion.3
  129.3 17.5 %all-gather.1 = bf16[512,128]{1,0:T(8,128)(2,1)S(1)} all-gather(bf16[64,128]{1,0:T(8,128)(2,1)S(1)} %copy.25), channel_id=3, replica_groups=mesh['gx'=8,'gy'=4] {'gx'}, dimensions={0}, use_global_device_ids=true | all-gather | bytes 147456 | tf_op jit(solution)/shard_map/all_gather | solution.py:174
  146.8 2.6 %collective-permute-start.7 = (bf16[64,2048]{1,0:T(8,128)(2,1)S(1)}, bf16[64,2048]{1,0:T(8,128)(2,1)S(1)}, u32[]{:S(2)}, u32[]{:S(2)}) collective-permute-start(bf16[64,2048]{1,0:T(8,128)(2,1)S(1)} %get-tuple-element.348), channel_id=1, source_target_pairs={{3,0},{4,1},{5,2},{6,3},{7,4},{8,5},{9,6},{10,7},{11,8},{12,9},{13... | collective-permute-start | bytes 786440 | tf_op jit(solution)/shard_map/ppermute | solution.py:17
  149.7 14.9 %all-gather = f32[256,128]{1,0:T(8,128)S(1)} all-gather(f32[32,128]{1,0:T(8,128)S(1)} %fusion.308), channel_id=2, replica_groups=mesh['gx'=8,'gy'=4] {'gx'}, dimensions={0}, use_global_device_ids=true | all-gather | bytes 147456 | tf_op jit(solution)/shard_map/all_gather | solution.py:180
  166.3 1.0 convolution_bitcast_fusion
  167.4 2.2 collective-permute-start.6
  171.1 0.4 fusion.201
  172.4 0.4 fusion.199
  173.6 0.4 fusion.197
  174.9 0.4 fusion.195
  175.5 0.4 fusion.194
  176.1 0.4 fusion.193
  177.4 1.9 collective-permute-start.10
  182.1 0.4 fusion.187
  182.7 0.4 fusion.186
  183.3 0.4 fusion.185
  184.6 0.4 fusion.183
  185.8 0.4 fusion.181
  186.4 0.4 fusion.180
  187.1 2.1 collective-permute-start.9
  190.1 0.4 fusion.178
  192.0 0.4 fusion.175
  192.6 0.4 fusion.174
  193.9 0.4 fusion.172
  194.5 0.4 fusion.171
  195.7 0.4 fusion.169
  196.4 0.4 fusion.168
  197.0 3.5 %collective-permute-start.2 = (f32[32,2048]{1,0:T(8,128)S(1)}, f32[32,2048]{1,0:T(8,128)S(1)}, u32[]{:S(2)}, u32[]{:S(2)}) collective-permute-start(f32[32,2048]{1,0:T(8,128)S(1)} %fusion.234), channel_id=1, source_target_pairs={{0,1},{1,2},{2,3},{3,4},{4,5},{5,6},{6,7},{7,8},{8,9},{9,10},{10,1... | collective-permute-start | bytes 786440 | tf_op jit(solution)/shard_map/ppermute | solution.py:17
  201.4 0.4 fusion.166
  202.1 0.4 fusion.165
  202.7 0.4 fusion.164
  203.3 0.4 fusion.163
  203.9 0.4 fusion.162
  204.6 0.4 fusion.161
  206.4 0.4 fusion.158
  207.7 0.4 fusion.156
  208.3 4.5 %collective-permute-start.5 = (f32[32,2048]{1,0:T(8,128)S(1)}, f32[32,2048]{1,0:T(8,128)S(1)}, u32[]{:S(2)}, u32[]{:S(2)}) collective-permute-start(f32[32,2048]{1,0:T(8,128)S(1)} %fusion.256), channel_id=1, source_target_pairs={{0,2},{1,3},{2,4},{3,5},{4,6},{5,7},{6,8},{7,9},{8,10},{9,11},{10,... | collective-permute-start | bytes 786440 | tf_op jit(solution)/shard_map/ppermute | solution.py:17
  216.1 3.4 %collective-permute-start.8 = (f32[32,2048]{1,0:T(8,128)S(1)}, f32[32,2048]{1,0:T(8,128)S(1)}, u32[]{:S(2)}, u32[]{:S(2)}) collective-permute-start(f32[32,2048]{1,0:T(8,128)S(1)} %fusion.278), channel_id=1, source_target_pairs={{0,3},{1,4},{2,5},{3,6},{4,7},{5,8},{6,9},{7,10},{8,11},{9,12},{10... | collective-permute-start | bytes 786440 | tf_op jit(solution)/shard_map/ppermute | solution.py:17
  219.6 3.3 %collective-permute-start.11 = (f32[32,2048]{1,0:T(8,128)S(1)}, f32[32,2048]{1,0:T(8,128)S(1)}, u32[]{:S(2)}, u32[]{:S(2)}) collective-permute-start(f32[32,2048]{1,0:T(8,128)S(1)} %fusion.300), channel_id=1, source_target_pairs={{0,4},{1,5},{2,6},{3,7},{4,8},{5,9},{6,10},{7,11},{8,12},{9,13},{1... | collective-permute-start | bytes 786440 | tf_op jit(solution)/shard_map/ppermute | solution.py:17
  232.7 0.8 add_add_fusion
  (204 shorter events, 36.5 us)
Async XLA Ops:
  0.0 12.6 %copy-start.4 = (s32[4,128]{1,0:T(4,128)S(1)}, s32[4,128]{1,0:T(4,128)}, u32[]{:S(2)}) copy-start(s32[4,128]{1,0:T(4,128)} %param.17) | copy-start | bytes 6148
  0.0 12.6 %copy-start.8 = (s32[1,128]{1,0:T(1,128)S(1)}, s32[1,128]{1,0:T(1,128)}, u32[]{:S(2)}) copy-start(s32[1,128]{1,0:T(1,128)} %param.19) | copy-start | bytes 1540
  0.0 167.4 %collective-permute-start.1 = (bf16[64,2048]{1,0:T(8,128)(2,1)}, bf16[64,2048]{1,0:T(8,128)(2,1)S(1)}, u32[]{:S(2)}, u32[]{:S(2)}) collective-permute-start(bf16[64,2048]{1,0:T(8,128)(2,1)} %param.15), channel_id=1, source_target_pairs={{1,0},{2,1},{3,2},{4,3},{5,4},{6,5},{7,6},{8,7},{9,8},{10,9},{11,1... | collective-permute-start | bytes 786440 | tf_op jit(solution)/shard_map/ppermute | solution.py:17
  3.2 174.2 %collective-permute-start.4 = (bf16[64,2048]{1,0:T(8,128)(2,1)}, bf16[64,2048]{1,0:T(8,128)(2,1)S(1)}, u32[]{:S(2)}, u32[]{:S(2)}) collective-permute-start(bf16[64,2048]{1,0:T(8,128)(2,1)} %param.15), channel_id=1, source_target_pairs={{2,0},{3,1},{4,2},{5,3},{6,4},{7,5},{8,6},{9,7},{10,8},{11,9},{12,... | collective-permute-start | bytes 786440 | tf_op jit(solution)/shard_map/ppermute | solution.py:17
  6.9 201.4 %collective-permute-start = (bf16[32,2048]{1,0:T(8,128)(2,1)}, bf16[32,2048]{1,0:T(8,128)(2,1)S(1)}, u32[]{:S(2)}, u32[]{:S(2)}) collective-permute-start(bf16[32,2048]{1,0:T(8,128)(2,1)} %param.16), channel_id=1, source_target_pairs={{1,0},{2,1},{3,2},{4,3},{5,4},{6,5},{7,6},{8,7},{9,8},{10,9},{11,1... | collective-permute-start | bytes 393224 | tf_op jit(solution)/shard_map/ppermute | solution.py:17
  9.4 210.2 %collective-permute-start.3 = (bf16[32,2048]{1,0:T(8,128)(2,1)}, bf16[32,2048]{1,0:T(8,128)(2,1)S(1)}, u32[]{:S(2)}, u32[]{:S(2)}) collective-permute-start(bf16[32,2048]{1,0:T(8,128)(2,1)} %param.16), channel_id=1, source_target_pairs={{2,0},{3,1},{4,2},{5,3},{6,4},{7,5},{8,6},{9,7},{10,8},{11,9},{12,... | collective-permute-start | bytes 393224 | tf_op jit(solution)/shard_map/ppermute | solution.py:17
  12.6 4.1 %copy-start.7 = (s32[1,3,128]{2,0,1:T(1,128)S(1)}, s32[1,3,128]{2,0,1:T(1,128)}, u32[]{:S(2)}) copy-start(s32[1,3,128]{2,0,1:T(1,128)} %param.21) | copy-start | bytes 4612
  12.6 5.7 %copy-start.2 = (s32[1,4,12]{2,1,0:T(4,128)S(1)}, s32[1,4,12]{2,1,0:T(4,128)}, u32[]{:S(2)}) copy-start(s32[1,4,12]{2,1,0:T(4,128)} %param.24) | copy-start | bytes 580
  12.7 6.9 %copy-start.3 = (s32[1,4,12]{2,1,0:T(4,128)S(1)}, s32[1,4,12]{2,1,0:T(4,128)}, u32[]{:S(2)}) copy-start(s32[1,4,12]{2,1,0:T(4,128)} %param.25) | copy-start | bytes 580
  16.8 105.3 %collective-permute-start.14 = (bf16[64,128]{0,1:T(8,128)(2,1)S(1)}, bf16[64,128]{0,1:T(8,128)(2,1)S(1)}, u32[]{:S(2)}, u32[]{:S(2)}) collective-permute-start(bf16[64,128]{0,1:T(8,128)(2,1)S(1)} %select_bitcast_fusion.1), channel_id=1, source_target_pairs={{0,1},{1,0},{2,3},{3,2},{4,5},{5,4},{6,7},{7,6},{8,9},{9,8},{10,11... | collective-permute-start | bytes 49160 | tf_op jit(solution)/shard_map/ppermute | solution.py:23
  28.6 84.1 %copy-start.6 = (s32[1,3,256]{2,0,1:T(1,128)S(1)}, s32[1,3,256]{2,0,1:T(1,128)}, u32[]{:S(2)}) copy-start(s32[1,3,256]{2,0,1:T(1,128)} %param.22) | copy-start | bytes 9220
  29.4 83.4 %copy-start.10 = (s32[1,8]{1,0:T(1,128)S(1)}, s32[1,8]{1,0:T(1,128)}, u32[]{:S(2)}) copy-start(s32[1,8]{1,0:T(1,128)} %param.23) | copy-start | bytes 100
  50.6 62.2 %copy-start = (bf16[64,2048]{1,0:T(8,128)(2,1)S(1)}, bf16[64,2048]{1,0:T(8,128)(2,1)}, u32[]{:S(2)}) copy-start(bf16[64,2048]{1,0:T(8,128)(2,1)} %param.15) | copy-start | bytes 786436
  50.6 62.2 %copy-start.1 = (bf16[32,2048]{1,0:T(8,128)(2,1)S(1)}, bf16[32,2048]{1,0:T(8,128)(2,1)}, u32[]{:S(2)}) copy-start(bf16[32,2048]{1,0:T(8,128)(2,1)} %param.16) | copy-start | bytes 393220
  112.8 6.7 %copy-start.9 = (s32[4,512]{1,0:T(4,128)S(1)}, s32[4,512]{1,0:T(4,128)}, u32[]{:S(2)}) copy-start(s32[4,512]{1,0:T(4,128)} %param.18) | copy-start | bytes 24580
  119.4 0.9 copy-start.5
  122.2 2.7 %collective-permute-start.12 = (f32[32,128]{1,0:T(8,128)S(1)}, f32[32,128]{1,0:T(8,128)S(1)}, u32[]{:S(2)}, u32[]{:S(2)}) collective-permute-start(f32[32,128]{1,0:T(8,128)S(1)} %fusion.303), channel_id=1, source_target_pairs={{0,1},{1,0},{2,3},{3,2},{4,5},{5,4},{6,7},{7,6},{8,9},{9,8},{10,11... | collective-permute-start | bytes 49160 | tf_op jit(solution)/shard_map/ppermute | solution.py:23
  124.8 2.8 %collective-permute-start.15 = (bf16[64,128]{0,1:T(8,128)(2,1)S(1)}, bf16[64,128]{0,1:T(8,128)(2,1)S(1)}, u32[]{:S(2)}, u32[]{:S(2)}) collective-permute-start(bf16[64,128]{0,1:T(8,128)(2,1)S(1)} %select_bitcast_fusion), channel_id=1, source_target_pairs={{0,2},{1,3},{2,0},{3,1},{4,6},{5,7},{6,4},{7,5},{8,10},{9,11},{10,... | collective-permute-start | bytes 49160 | tf_op jit(solution)/shard_map/ppermute | solution.py:23
  127.6 19.2 %collective-permute-start.13 = (f32[32,128]{1,0:T(8,128)S(1)}, f32[32,128]{1,0:T(8,128)S(1)}, u32[]{:S(2)}, u32[]{:S(2)}) collective-permute-start(f32[32,128]{1,0:T(8,128)S(1)} %fusion.310), channel_id=1, source_target_pairs={{0,2},{1,3},{2,0},{3,1},{4,6},{5,7},{6,4},{7,5},{8,10},{9,11},{10,... | collective-permute-start | bytes 49160 | tf_op jit(solution)/shard_map/ppermute | solution.py:23
  146.8 40.2 %collective-permute-start.7 = (bf16[64,2048]{1,0:T(8,128)(2,1)S(1)}, bf16[64,2048]{1,0:T(8,128)(2,1)S(1)}, u32[]{:S(2)}, u32[]{:S(2)}) collective-permute-start(bf16[64,2048]{1,0:T(8,128)(2,1)S(1)} %get-tuple-element.348), channel_id=1, source_target_pairs={{3,0},{4,1},{5,2},{6,3},{7,4},{8,5},{9,6},{10,7},{11,8},{12,9},{13... | collective-permute-start | bytes 786440 | tf_op jit(solution)/shard_map/ppermute | solution.py:17
  167.4 58.8 %collective-permute-start.6 = (bf16[32,2048]{1,0:T(8,128)(2,1)S(1)}, bf16[32,2048]{1,0:T(8,128)(2,1)S(1)}, u32[]{:S(2)}, u32[]{:S(2)}) collective-permute-start(bf16[32,2048]{1,0:T(8,128)(2,1)S(1)} %get-tuple-element.353), channel_id=1, source_target_pairs={{3,0},{4,1},{5,2},{6,3},{7,4},{8,5},{9,6},{10,7},{11,8},{12,9},{13... | collective-permute-start | bytes 393224 | tf_op jit(solution)/shard_map/ppermute | solution.py:17
  177.4 19.6 %collective-permute-start.10 = (bf16[64,2048]{1,0:T(8,128)(2,1)S(1)}, bf16[64,2048]{1,0:T(8,128)(2,1)S(1)}, u32[]{:S(2)}, u32[]{:S(2)}) collective-permute-start(bf16[64,2048]{1,0:T(8,128)(2,1)S(1)} %get-tuple-element.348), channel_id=1, source_target_pairs={{4,0},{5,1},{6,2},{7,3},{8,4},{9,5},{10,6},{11,7},{12,8},{13,9},{1... | collective-permute-start | bytes 786440 | tf_op jit(solution)/shard_map/ppermute | solution.py:17
  187.1 42.4 %collective-permute-start.9 = (bf16[32,2048]{1,0:T(8,128)(2,1)S(1)}, bf16[32,2048]{1,0:T(8,128)(2,1)S(1)}, u32[]{:S(2)}, u32[]{:S(2)}) collective-permute-start(bf16[32,2048]{1,0:T(8,128)(2,1)S(1)} %get-tuple-element.353), channel_id=1, source_target_pairs={{4,0},{5,1},{6,2},{7,3},{8,4},{9,5},{10,6},{11,7},{12,8},{13,9},{1... | collective-permute-start | bytes 393224 | tf_op jit(solution)/shard_map/ppermute | solution.py:17
  197.0 19.1 %collective-permute-start.2 = (f32[32,2048]{1,0:T(8,128)S(1)}, f32[32,2048]{1,0:T(8,128)S(1)}, u32[]{:S(2)}, u32[]{:S(2)}) collective-permute-start(f32[32,2048]{1,0:T(8,128)S(1)} %fusion.234), channel_id=1, source_target_pairs={{0,1},{1,2},{2,3},{3,4},{4,5},{5,6},{6,7},{7,8},{8,9},{9,10},{10,1... | collective-permute-start | bytes 786440 | tf_op jit(solution)/shard_map/ppermute | solution.py:17
  208.3 17.8 %collective-permute-start.5 = (f32[32,2048]{1,0:T(8,128)S(1)}, f32[32,2048]{1,0:T(8,128)S(1)}, u32[]{:S(2)}, u32[]{:S(2)}) collective-permute-start(f32[32,2048]{1,0:T(8,128)S(1)} %fusion.256), channel_id=1, source_target_pairs={{0,2},{1,3},{2,4},{3,5},{4,6},{5,7},{6,8},{7,9},{8,10},{9,11},{10,... | collective-permute-start | bytes 786440 | tf_op jit(solution)/shard_map/ppermute | solution.py:17
  216.1 13.3 %collective-permute-start.8 = (f32[32,2048]{1,0:T(8,128)S(1)}, f32[32,2048]{1,0:T(8,128)S(1)}, u32[]{:S(2)}, u32[]{:S(2)}) collective-permute-start(f32[32,2048]{1,0:T(8,128)S(1)} %fusion.278), channel_id=1, source_target_pairs={{0,3},{1,4},{2,5},{3,6},{4,7},{5,8},{6,9},{7,10},{8,11},{9,12},{10... | collective-permute-start | bytes 786440 | tf_op jit(solution)/shard_map/ppermute | solution.py:17
  219.6 13.1 %collective-permute-start.11 = (f32[32,2048]{1,0:T(8,128)S(1)}, f32[32,2048]{1,0:T(8,128)S(1)}, u32[]{:S(2)}, u32[]{:S(2)}) collective-permute-start(f32[32,2048]{1,0:T(8,128)S(1)} %fusion.300), channel_id=1, source_target_pairs={{0,4},{1,5},{2,6},{3,7},{4,8},{5,9},{6,10},{7,11},{8,12},{9,13},{1... | collective-permute-start | bytes 786440 | tf_op jit(solution)/shard_map/ppermute | solution.py:17
where the time goes:
time: 235 us; the launch traced here: 233 us
  between operations  92.5 us (39%)
  matrix products  51.8 us (22%)
  starting transfers between devices  37.5 us (16%)
  blocking collectives  32.5 us (14%)
  local copies, waits for them, and re-layouts  11.1 us (5%)
  waiting for transfers between devices  4.06 us (2%)
  other arithmetic  3.96 us (2%)
    ppermute x12, starting transfers between devices, passed_along(): lax.ppermute(value, axis, [(source, source + steps) for source in range(f...  34.9 us
    dot_general x49, matrix products, kernel_block(): lax.dot_general(source, target, (((0,), (0,)), ((), ())), preferred_eleme...  20.8 us
    all_gather x1, blocking collectives, on_device(): gathered_roots = lax.all_gather(node_points[None], 'gx', axis=0, tiled=True)  17.5 us
    all_gather x1, blocking collectives, on_device(): lax.all_gather(node_weights[None], 'gx', axis=0, tiled=True)  14.9 us
    dot_general x48, matrix products, pair_terms(): lax.dot_general(high_values, kernel_tile, (((1,), (1,)), ((), ())), prefe...  12.2 us
    dot_general x48, matrix products, pair_terms(): jnp.dot(low_values, kernel_tile, preferred_element_type=jnp.float32)  9.1 us
    dot_general x4, matrix products, self_target(): jnp.dot(vectors, kernel_tile, preferred_element_type=jnp.float32)  6.01 us
  transfers between devices with their start and end apart: 16, of which 2 were waited for; matrix products, arithmetic and copies ran while one was open for 28% of the time, Pallas kernels for 0%

commit v1 on v0

--- a/solution.py
+++ b/solution.py
@@ -9,6 +9,12 @@
 SKEL = 128
 LPD = 4
 KERNEL_RATE = 2.0
+assign_loads = lambda sheet, axis_key, array_axis: jnp.concatenate(
+    jax.lax.all_to_all(
+        jnp.stack([sheet for _ in range(jax.lax.axis_size(axis_key))]), axis_key, 0, 0
+    ),
+    array_axis,
+)
 
 
 def passed_along(value, axis, steps):
@@ -177,7 +183,7 @@
     node_potential = jnp.einsum(
         "n,ncs,nst->ct",
         far_flags,
-        lax.all_gather(node_weights[None], "gx", axis=0, tiled=True),
+        assign_loads(node_weights[None], "gx", 0),
         root_kernels,
         precision=lax.Precision.HIGHEST,
     )

time: 235 us -> 233 us (level)
  blocking collectives: 32.5 us -> 17.5 us
  waiting for transfers between devices: 4.06 us -> 9.48 us
  starting transfers between devices: 37.5 us -> 42.8 us
    all_gather x1 -> x0, blocking collectives: 14.9 us -> none  [on_device(): lax.all_gather(node_weights[None], 'gx', axis=0, tiled=True)]
    all_to_all x0 -> x1, waiting for transfers between devices: none -> 5.42 us  [jax.lax.all_to_all(jnp.stack([sheet for _ in range(jax.lax.axis_size(axis...]
    all_to_all x0 -> x1, starting transfers between devices: none -> 4.71 us  [jax.lax.all_to_all(jnp.stack([sheet for _ in range(jax.lax.axis_size(axis...]
  transfers between devices with their start and end apart: 16 -> 17, of which waited for: 2 -> 3; matrix products, arithmetic and copies ran while one was open for 28% -> 29% of each run, Pallas kernels for 0% -> 0%
where the time goes in v1:
time: 233 us; the launch traced here: 230 us
  between operations  92.5 us (40%)
  matrix products  51.8 us (22%)
  starting transfers between devices  42.8 us (18%)
  blocking collectives  17.5 us (8%)
  local copies, waits for them, and re-layouts  11.8 us (5%)
  waiting for transfers between devices  9.48 us (4%)
  other arithmetic  3.96 us (2%)
    ppermute x12, starting transfers between devices, passed_along(): lax.ppermute(value, axis, [(source, source + steps) for source in range(f...  35.6 us
    dot_general x49, matrix products, kernel_block(): lax.dot_general(source, target, (((0,), (0,)), ((), ())), preferred_eleme...  20.7 us
    all_gather x1, blocking collectives, on_device(): gathered_roots = lax.all_gather(node_points[None], 'gx', axis=0, tiled=True)  17.5 us
    dot_general x48, matrix products, pair_terms(): lax.dot_general(high_values, kernel_tile, (((1,), (1,)), ((), ())), prefe...  12.2 us
    dot_general x48, matrix products, pair_terms(): jnp.dot(low_values, kernel_tile, preferred_element_type=jnp.float32)  9.11 us
    dot_general x4, matrix products, self_target(): jnp.dot(vectors, kernel_tile, preferred_element_type=jnp.float32)  6.01 us
    all_to_all x1, waiting for transfers between devices, jax.lax.all_to_all(jnp.stack([sheet for _ in range(jax.lax.axis_size(axis...  5.42 us
    all_to_all x1, starting transfers between devices, jax.lax.all_to_all(jnp.stack([sheet for _ in range(jax.lax.axis_size(axis...  4.71 us
  transfers between devices with their start and end apart: 17, of which 3 were waited for; matrix products, arithmetic and copies ran while one was open for 29% of the time, Pallas kernels for 0%

profile of v1, /device:TPU:5, one launch (start us, length us, event | category | flops | bytes accessed | tf_op | source)
XLA Modules:
  0.0 229.9 jit_solution(6906976321797699625)
XLA Ops:
  0.0 3.2 %collective-permute-start.1 = (bf16[64,2048]{1,0:T(8,128)(2,1)}, bf16[64,2048]{1,0:T(8,128)(2,1)S(1)}, u32[]{:S(2)}, u32[]{:S(2)}) collective-permute-start(bf16[64,2048]{1,0:T(8,128)(2,1)} %param.15), channel_id=1, source_target_pairs={{1,0},{2,1},{3,2},{4,3},{5,4},{6,5},{7,6},{8,7},{9,8},{10,9},{11,1... | collective-permute-start | bytes 786440 | tf_op jit(solution)/shard_map/ppermute | solution.py:23
  3.2 3.7 %collective-permute-start.4 = (bf16[64,2048]{1,0:T(8,128)(2,1)}, bf16[64,2048]{1,0:T(8,128)(2,1)S(1)}, u32[]{:S(2)}, u32[]{:S(2)}) collective-permute-start(bf16[64,2048]{1,0:T(8,128)(2,1)} %param.15), channel_id=1, source_target_pairs={{2,0},{3,1},{4,2},{5,3},{6,4},{7,5},{8,6},{9,7},{10,8},{11,9},{12,... | collective-permute-start | bytes 786440 | tf_op jit(solution)/shard_map/ppermute | solution.py:23
  6.9 2.4 %collective-permute-start = (bf16[32,2048]{1,0:T(8,128)(2,1)}, bf16[32,2048]{1,0:T(8,128)(2,1)S(1)}, u32[]{:S(2)}, u32[]{:S(2)}) collective-permute-start(bf16[32,2048]{1,0:T(8,128)(2,1)} %param.16), channel_id=1, source_target_pairs={{1,0},{2,1},{3,2},{4,3},{5,4},{6,5},{7,6},{8,7},{9,8},{10,9},{11,1... | collective-permute-start | bytes 393224 | tf_op jit(solution)/shard_map/ppermute | solution.py:23
  9.4 1.9 collective-permute-start.3
  11.3 1.2 copy.31
  12.7 3.2 %gather_fusion.1 = bf16[512,64]{1,0:T(8,128)(2,1)S(1)} fusion(bf16[4,64,512]{1,2,0:T(8,128)(2,1)S(1)} %bitcast.343, s32[512]{0:T(512)S(1)} %fusion.382), kind=kCustom, calls=%fused_computation.3 | custom fusion | bytes 135168 | tf_op jit(solution)/shard_map/vmap(jit(_take))/gather | solution.py:50
  16.0 0.7 gather_fusion
  16.8 1.5 collective-permute-start.14
  18.3 0.7 fusion.395
  19.6 0.7 fusion.391
  22.3 0.7 fusion.392
  28.6 0.7 fusion.394
  52.0 0.7 fusion.393
  70.5 0.7 fusion.390
  112.8 6.5 %while.13 = (s32[]{:T(128)}, f32[32,2048]{1,0:T(8,128)S(1)}, bf16[64,2048]{1,0:T(8,128)(2,1)S(1)}, bf16[32,2048]{1,0:T(8,128)(2,1)S(1)}, s32[]{:T(128)}, /*index=5*/s32[]{:T(128)}, s32[]{:T(128)}, s32[]{:T(128)}) while((s32[]{:T(128)}, f32[32,2048]{1,0:T(8,128)S(1)}, bf16[64,2048]{1,0:T(8,128)(2,1)S(1)}, bf16[32,2048]{1,0:T(8,128)(2,1)S(1)}, ...), condition=%wide.region_3.0_spmd, body=%wide.region_0.0_spmd.sunk | while | flops 207058432 | bytes 873615 | solution.py:123
  112.9 1.5 fusion.504
  114.6 1.5 fusion.504
  116.2 1.5 fusion.504
  117.8 1.5 fusion.504
  119.5 0.7 convolution_bitcast_fusion.2
  122.3 0.7 gather_fusion.2
  123.1 1.7 collective-permute-done.12
  125.3 2.2 collective-permute-done.15
  127.6 0.7 collective-permute-start.13
  128.2 0.7 gather_fusion.3
  129.2 17.5 %all-gather = bf16[512,128]{1,0:T(8,128)(2,1)S(1)} all-gather(bf16[64,128]{1,0:T(8,128)(2,1)S(1)} %copy.32), channel_id=2, replica_groups=mesh['gx'=8,'gy'=4] {'gx'}, dimensions={0}, use_global_device_ids=true | all-gather | bytes 147456 | tf_op jit(solution)/shard_map/all_gather | solution.py:180
  146.8 2.6 %collective-permute-start.7 = (bf16[64,2048]{1,0:T(8,128)(2,1)S(1)}, bf16[64,2048]{1,0:T(8,128)(2,1)S(1)}, u32[]{:S(2)}, u32[]{:S(2)}) collective-permute-start(bf16[64,2048]{1,0:T(8,128)(2,1)S(1)} %get-tuple-element.348), channel_id=1, source_target_pairs={{3,0},{4,1},{5,2},{6,3},{7,4},{8,5},{9,6},{10,7},{11,8},{12,9},{13... | collective-permute-start | bytes 786440 | tf_op jit(solution)/shard_map/ppermute | solution.py:23
  149.6 0.7 stack.3
  150.3 4.7 %all-to-all-start = ((f32[8,1,32,128]{3,2,1,0:T(8,128)}), f32[8,1,32,128]{3,2,1,0:T(8,128)S(1)}, u32[]{:S(2)}, u32[]{:S(2)}) async-start(f32[8,1,32,128]{3,2,1,0:T(8,128)} %stack.3), calls=%async_computation | async-start | bytes 262144 | tf_op jit(solution)/shard_map/all_to_all | solution.py:13
  155.4 5.4 %all-to-all-done = f32[8,1,32,128]{3,2,1,0:T(8,128)S(1)} async-done(((f32[8,1,32,128]{3,2,1,0:T(8,128)}), f32[8,1,32,128]{3,2,1,0:T(8,128)S(1)}, u32[]{:S(2)}, u32[]{:S(2)}) %all-to-all-start) | async-done | bytes 131104 | tf_op jit(solution)/shard_map/all_to_all | solution.py:13
  161.5 4.0 %collective-permute-start.6 = (bf16[32,2048]{1,0:T(8,128)(2,1)S(1)}, bf16[32,2048]{1,0:T(8,128)(2,1)S(1)}, u32[]{:S(2)}, u32[]{:S(2)}) collective-permute-start(bf16[32,2048]{1,0:T(8,128)(2,1)S(1)} %get-tuple-element.353), channel_id=1, source_target_pairs={{3,0},{4,1},{5,2},{6,3},{7,4},{8,5},{9,6},{10,7},{11,8},{12,9},{13... | collective-permute-start | bytes 393224 | tf_op jit(solution)/shard_map/ppermute | solution.py:23
  166.4 0.4 fusion.202
  167.7 0.4 fusion.200
  168.9 0.4 fusion.198
  169.5 0.4 fusion.197
  170.2 0.4 fusion.196
  171.4 0.4 fusion.194
  172.0 0.4 fusion.193
  173.6 1.9 collective-permute-start.10
  176.4 0.4 fusion.190
  177.0 0.4 fusion.189
  177.6 0.4 fusion.188
  178.9 0.4 fusion.186
  180.8 0.4 fusion.183
  182.6 0.4 fusion.180
  183.6 2.1 collective-permute-start.9
  187.3 0.4 fusion.177
  187.9 0.4 fusion.176
  189.1 0.4 fusion.174
  189.8 0.4 fusion.173
  190.4 0.4 fusion.172
  192.3 0.4 fusion.169
  192.9 0.4 fusion.168
  193.3 1.0 convolution_bitcast_fusion
  194.6 2.1 collective-permute-start.2
  197.6 0.4 fusion.166
  198.3 0.4 fusion.165
  198.9 0.4 fusion.164
  200.8 0.4 fusion.161
  201.4 0.4 fusion.160
  204.5 5.0 %collective-permute-start.5 = (f32[32,2048]{1,0:T(8,128)S(1)}, f32[32,2048]{1,0:T(8,128)S(1)}, u32[]{:S(2)}, u32[]{:S(2)}) collective-permute-start(f32[32,2048]{1,0:T(8,128)S(1)} %fusion.256), channel_id=1, source_target_pairs={{0,2},{1,3},{2,4},{3,5},{4,6},{5,7},{6,8},{7,9},{8,10},{9,11},{10,... | collective-permute-start | bytes 786440 | tf_op jit(solution)/shard_map/ppermute | solution.py:23
  212.8 4.0 %collective-permute-start.8 = (f32[32,2048]{1,0:T(8,128)S(1)}, f32[32,2048]{1,0:T(8,128)S(1)}, u32[]{:S(2)}, u32[]{:S(2)}) collective-permute-start(f32[32,2048]{1,0:T(8,128)S(1)} %fusion.278), channel_id=1, source_target_pairs={{0,3},{1,4},{2,5},{3,6},{4,7},{5,8},{6,9},{7,10},{8,11},{9,12},{10... | collective-permute-start | bytes 786440 | tf_op jit(solution)/shard_map/ppermute | solution.py:23
  216.9 2.5 %collective-permute-start.11 = (f32[32,2048]{1,0:T(8,128)S(1)}, f32[32,2048]{1,0:T(8,128)S(1)}, u32[]{:S(2)}, u32[]{:S(2)}) collective-permute-start(f32[32,2048]{1,0:T(8,128)S(1)} %fusion.300), channel_id=1, source_target_pairs={{0,4},{1,5},{2,6},{3,7},{4,8},{5,9},{6,10},{7,11},{8,12},{9,13},{1... | collective-permute-start | bytes 786440 | tf_op jit(solution)/shard_map/ppermute | solution.py:23
  229.2 0.8 add_add_fusion
  (206 shorter events, 37.4 us)
Async XLA Ops:
  0.0 12.6 %copy-start.4 = (s32[4,128]{1,0:T(4,128)S(1)}, s32[4,128]{1,0:T(4,128)}, u32[]{:S(2)}) copy-start(s32[4,128]{1,0:T(4,128)} %param.17) | copy-start | bytes 6148
  0.0 12.6 %copy-start.8 = (s32[1,128]{1,0:T(1,128)S(1)}, s32[1,128]{1,0:T(1,128)}, u32[]{:S(2)}) copy-start(s32[1,128]{1,0:T(1,128)} %param.19) | copy-start | bytes 1540
  0.0 161.5 %collective-permute-start.1 = (bf16[64,2048]{1,0:T(8,128)(2,1)}, bf16[64,2048]{1,0:T(8,128)(2,1)S(1)}, u32[]{:S(2)}, u32[]{:S(2)}) collective-permute-start(bf16[64,2048]{1,0:T(8,128)(2,1)} %param.15), channel_id=1, source_target_pairs={{1,0},{2,1},{3,2},{4,3},{5,4},{6,5},{7,6},{8,7},{9,8},{10,9},{11,1... | collective-permute-start | bytes 786440 | tf_op jit(solution)/shard_map/ppermute | solution.py:23
  3.2 170.4 %collective-permute-start.4 = (bf16[64,2048]{1,0:T(8,128)(2,1)}, bf16[64,2048]{1,0:T(8,128)(2,1)S(1)}, u32[]{:S(2)}, u32[]{:S(2)}) collective-permute-start(bf16[64,2048]{1,0:T(8,128)(2,1)} %param.15), channel_id=1, source_target_pairs={{2,0},{3,1},{4,2},{5,3},{6,4},{7,5},{8,6},{9,7},{10,8},{11,9},{12,... | collective-permute-start | bytes 786440 | tf_op jit(solution)/shard_map/ppermute | solution.py:23
  6.9 197.6 %collective-permute-start = (bf16[32,2048]{1,0:T(8,128)(2,1)}, bf16[32,2048]{1,0:T(8,128)(2,1)S(1)}, u32[]{:S(2)}, u32[]{:S(2)}) collective-permute-start(bf16[32,2048]{1,0:T(8,128)(2,1)} %param.16), channel_id=1, source_target_pairs={{1,0},{2,1},{3,2},{4,3},{5,4},{6,5},{7,6},{8,7},{9,8},{10,9},{11,1... | collective-permute-start | bytes 393224 | tf_op jit(solution)/shard_map/ppermute | solution.py:23
  9.4 207.5 %collective-permute-start.3 = (bf16[32,2048]{1,0:T(8,128)(2,1)}, bf16[32,2048]{1,0:T(8,128)(2,1)S(1)}, u32[]{:S(2)}, u32[]{:S(2)}) collective-permute-start(bf16[32,2048]{1,0:T(8,128)(2,1)} %param.16), channel_id=1, source_target_pairs={{2,0},{3,1},{4,2},{5,3},{6,4},{7,5},{8,6},{9,7},{10,8},{11,9},{12,... | collective-permute-start | bytes 393224 | tf_op jit(solution)/shard_map/ppermute | solution.py:23
  12.6 4.1 %copy-start.7 = (s32[1,3,128]{2,0,1:T(1,128)S(1)}, s32[1,3,128]{2,0,1:T(1,128)}, u32[]{:S(2)}) copy-start(s32[1,3,128]{2,0,1:T(1,128)} %param.21) | copy-start | bytes 4612
  12.6 5.7 %copy-start.2 = (s32[1,4,12]{2,1,0:T(4,128)S(1)}, s32[1,4,12]{2,1,0:T(4,128)}, u32[]{:S(2)}) copy-start(s32[1,4,12]{2,1,0:T(4,128)} %param.24) | copy-start | bytes 580
  12.7 6.9 %copy-start.3 = (s32[1,4,12]{2,1,0:T(4,128)S(1)}, s32[1,4,12]{2,1,0:T(4,128)}, u32[]{:S(2)}) copy-start(s32[1,4,12]{2,1,0:T(4,128)} %param.25) | copy-start | bytes 580
  16.8 105.3 %collective-permute-start.14 = (bf16[64,128]{0,1:T(8,128)(2,1)S(1)}, bf16[64,128]{0,1:T(8,128)(2,1)S(1)}, u32[]{:S(2)}, u32[]{:S(2)}) collective-permute-start(bf16[64,128]{0,1:T(8,128)(2,1)S(1)} %select_bitcast_fusion.1), channel_id=1, source_target_pairs={{0,1},{1,0},{2,3},{3,2},{4,5},{5,4},{6,7},{7,6},{8,9},{9,8},{10,11... | collective-permute-start | bytes 49160 | tf_op jit(solution)/shard_map/ppermute | solution.py:29
  28.6 84.0 %copy-start.6 = (s32[1,3,256]{2,0,1:T(1,128)S(1)}, s32[1,3,256]{2,0,1:T(1,128)}, u32[]{:S(2)}) copy-start(s32[1,3,256]{2,0,1:T(1,128)} %param.22) | copy-start | bytes 9220
  29.4 83.4 %copy-start.10 = (s32[1,8]{1,0:T(1,128)S(1)}, s32[1,8]{1,0:T(1,128)}, u32[]{:S(2)}) copy-start(s32[1,8]{1,0:T(1,128)} %param.23) | copy-start | bytes 100
  50.6 62.2 %copy-start = (bf16[64,2048]{1,0:T(8,128)(2,1)S(1)}, bf16[64,2048]{1,0:T(8,128)(2,1)}, u32[]{:S(2)}) copy-start(bf16[64,2048]{1,0:T(8,128)(2,1)} %param.15) | copy-start | bytes 786436
  50.6 62.2 %copy-start.1 = (bf16[32,2048]{1,0:T(8,128)(2,1)S(1)}, bf16[32,2048]{1,0:T(8,128)(2,1)}, u32[]{:S(2)}) copy-start(bf16[32,2048]{1,0:T(8,128)(2,1)} %param.16) | copy-start | bytes 393220
  112.8 6.7 %copy-start.9 = (s32[4,512]{1,0:T(4,128)S(1)}, s32[4,512]{1,0:T(4,128)}, u32[]{:S(2)}) copy-start(s32[4,512]{1,0:T(4,128)} %param.18) | copy-start | bytes 24580
  119.3 0.9 copy-start.5
  122.1 2.7 %collective-permute-start.12 = (f32[32,128]{1,0:T(8,128)S(1)}, f32[32,128]{1,0:T(8,128)S(1)}, u32[]{:S(2)}, u32[]{:S(2)}) collective-permute-start(f32[32,128]{1,0:T(8,128)S(1)} %fusion.303), channel_id=1, source_target_pairs={{0,1},{1,0},{2,3},{3,2},{4,5},{5,4},{6,7},{7,6},{8,9},{9,8},{10,11... | collective-permute-start | bytes 49160 | tf_op jit(solution)/shard_map/ppermute | solution.py:29
  124.8 2.8 %collective-permute-start.15 = (bf16[64,128]{0,1:T(8,128)(2,1)S(1)}, bf16[64,128]{0,1:T(8,128)(2,1)S(1)}, u32[]{:S(2)}, u32[]{:S(2)}) collective-permute-start(bf16[64,128]{0,1:T(8,128)(2,1)S(1)} %select_bitcast_fusion), channel_id=1, source_target_pairs={{0,2},{1,3},{2,0},{3,1},{4,6},{5,7},{6,4},{7,5},{8,10},{9,11},{10,... | collective-permute-start | bytes 49160 | tf_op jit(solution)/shard_map/ppermute | solution.py:29
  127.6 19.3 %collective-permute-start.13 = (f32[32,128]{1,0:T(8,128)S(1)}, f32[32,128]{1,0:T(8,128)S(1)}, u32[]{:S(2)}, u32[]{:S(2)}) collective-permute-start(f32[32,128]{1,0:T(8,128)S(1)} %fusion.309), channel_id=1, source_target_pairs={{0,2},{1,3},{2,0},{3,1},{4,6},{5,7},{6,4},{7,5},{8,10},{9,11},{10,... | collective-permute-start | bytes 49160 | tf_op jit(solution)/shard_map/ppermute | solution.py:29
  146.8 36.8 %collective-permute-start.7 = (bf16[64,2048]{1,0:T(8,128)(2,1)S(1)}, bf16[64,2048]{1,0:T(8,128)(2,1)S(1)}, u32[]{:S(2)}, u32[]{:S(2)}) collective-permute-start(bf16[64,2048]{1,0:T(8,128)(2,1)S(1)} %get-tuple-element.348), channel_id=1, source_target_pairs={{3,0},{4,1},{5,2},{6,3},{7,4},{8,5},{9,6},{10,7},{11,8},{12,9},{13... | collective-permute-start | bytes 786440 | tf_op jit(solution)/shard_map/ppermute | solution.py:23
  150.3 10.5 %all-to-all-start = ((f32[8,1,32,128]{3,2,1,0:T(8,128)}), f32[8,1,32,128]{3,2,1,0:T(8,128)S(1)}, u32[]{:S(2)}, u32[]{:S(2)}) async-start(f32[8,1,32,128]{3,2,1,0:T(8,128)} %stack.3), calls=%async_computation | async-start | bytes 262144 | tf_op jit(solution)/shard_map/all_to_all | solution.py:13
  161.5 61.1 %collective-permute-start.6 = (bf16[32,2048]{1,0:T(8,128)(2,1)S(1)}, bf16[32,2048]{1,0:T(8,128)(2,1)S(1)}, u32[]{:S(2)}, u32[]{:S(2)}) collective-permute-start(bf16[32,2048]{1,0:T(8,128)(2,1)S(1)} %get-tuple-element.353), channel_id=1, source_target_pairs={{3,0},{4,1},{5,2},{6,3},{7,4},{8,5},{9,6},{10,7},{11,8},{12,9},{13... | collective-permute-start | bytes 393224 | tf_op jit(solution)/shard_map/ppermute | solution.py:23
  173.6 21.0 %collective-permute-start.10 = (bf16[64,2048]{1,0:T(8,128)(2,1)S(1)}, bf16[64,2048]{1,0:T(8,128)(2,1)S(1)}, u32[]{:S(2)}, u32[]{:S(2)}) collective-permute-start(bf16[64,2048]{1,0:T(8,128)(2,1)S(1)} %get-tuple-element.348), channel_id=1, source_target_pairs={{4,0},{5,1},{6,2},{7,3},{8,4},{9,5},{10,6},{11,7},{12,8},{13,9},{1... | collective-permute-start | bytes 786440 | tf_op jit(solution)/shard_map/ppermute | solution.py:23
  183.6 42.3 %collective-permute-start.9 = (bf16[32,2048]{1,0:T(8,128)(2,1)S(1)}, bf16[32,2048]{1,0:T(8,128)(2,1)S(1)}, u32[]{:S(2)}, u32[]{:S(2)}) collective-permute-start(bf16[32,2048]{1,0:T(8,128)(2,1)S(1)} %get-tuple-element.353), channel_id=1, source_target_pairs={{4,0},{5,1},{6,2},{7,3},{8,4},{9,5},{10,6},{11,7},{12,8},{13,9},{1... | collective-permute-start | bytes 393224 | tf_op jit(solution)/shard_map/ppermute | solution.py:23
  194.6 18.1 %collective-permute-start.2 = (f32[32,2048]{1,0:T(8,128)S(1)}, f32[32,2048]{1,0:T(8,128)S(1)}, u32[]{:S(2)}, u32[]{:S(2)}) collective-permute-start(f32[32,2048]{1,0:T(8,128)S(1)} %fusion.234), channel_id=1, source_target_pairs={{0,1},{1,2},{2,3},{3,4},{4,5},{5,6},{6,7},{7,8},{8,9},{9,10},{10,1... | collective-permute-start | bytes 786440 | tf_op jit(solution)/shard_map/ppermute | solution.py:23
  204.5 18.1 %collective-permute-start.5 = (f32[32,2048]{1,0:T(8,128)S(1)}, f32[32,2048]{1,0:T(8,128)S(1)}, u32[]{:S(2)}, u32[]{:S(2)}) collective-permute-start(f32[32,2048]{1,0:T(8,128)S(1)} %fusion.256), channel_id=1, source_target_pairs={{0,2},{1,3},{2,4},{3,5},{4,6},{5,7},{6,8},{7,9},{8,10},{9,11},{10,... | collective-permute-start | bytes 786440 | tf_op jit(solution)/shard_map/ppermute | solution.py:23
  212.8 13.1 %collective-permute-start.8 = (f32[32,2048]{1,0:T(8,128)S(1)}, f32[32,2048]{1,0:T(8,128)S(1)}, u32[]{:S(2)}, u32[]{:S(2)}) collective-permute-start(f32[32,2048]{1,0:T(8,128)S(1)} %fusion.278), channel_id=1, source_target_pairs={{0,3},{1,4},{2,5},{3,6},{4,7},{5,8},{6,9},{7,10},{8,11},{9,12},{10... | collective-permute-start | bytes 786440 | tf_op jit(solution)/shard_map/ppermute | solution.py:23
  216.9 12.3 %collective-permute-start.11 = (f32[32,2048]{1,0:T(8,128)S(1)}, f32[32,2048]{1,0:T(8,128)S(1)}, u32[]{:S(2)}, u32[]{:S(2)}) collective-permute-start(f32[32,2048]{1,0:T(8,128)S(1)} %fusion.300), channel_id=1, source_target_pairs={{0,4},{1,5},{2,6},{3,7},{4,8},{5,9},{6,10},{7,11},{8,12},{9,13},{1... | collective-permute-start | bytes 786440 | tf_op jit(solution)/shard_map/ppermute | solution.py:23
